TPU v7x, 256 devices: a whole 4x4x8 slice. The times are simulated.
256 devices in a mesh: dp: 64 (over z, y, core), tp: 4 (over x).
Axes of the slice: x: 4, y: 4, z: 8, core: 2. Of those that a mesh axis runs over, the one named last changes fastest.
Arguments:
- attn_partial: bfloat16 [4, 4096, 7168], P('tp', 'dp'), may hold values from -3 to 3
- hidden_in: bfloat16 [4096, 7168], P('dp', 'tp'), may hold values from -6 to 6
- norm_gain: float32 [7168], replicated, may hold values from 0.5 to 1.5
- expert_ids: int32 [4096, 8], P('dp'), may hold values from 0 to 255, all different within a row; in each aligned block of 64 rows (0 to 63, 64 to 127, ...) at most 4 rows name the same one
- route_prob: bfloat16 [4096, 8], P('dp'), may hold values from 0.049804688 to 0.3984375
- w_gate: bfloat16 [64, 7168, 1024], P('dp', None, 'tp'), may hold values from -0.0625 to 0.0625
- w_up: bfloat16 [64, 7168, 1024], P('dp', None, 'tp'), may hold values from -0.0625 to 0.0625
- w_down: bfloat16 [64, 1024, 7168], P('dp', 'tp'), may hold values from -0.1875 to 0.1875
Outputs:
- layer_out: bfloat16 [4096, 7168], P('dp', 'tp')
- amax_input: float32 [64], P('dp')
- amax_hidden: float32 [64], P('dp')
Inputs may be any that keep to these rules, and one draw needn't show every extreme that they name: `expert_ids`: each token names 8 different experts; within each aligned block of 64 tokens no expert is named by more than 4 tokens.
All inputs are finite; a program needn't handle non-finite values.
Results may differ from a plain program's by a relative error of at most 0.0075.
Values may be sent and summed in bfloat16 or wider, within the bound.
A program may use at most 64 MiB of HBM per device.

v0:
```python
import jax
import jax.numpy as jnp
from jax import lax
from jax.sharding import PartitionSpec as P

EXPERT_SLOTS = 4
eps = 1e-06


def route_tables(expert_ids, route_prob, experts, capacity):
    matches = expert_ids[:, :, None] == jnp.arange(experts, dtype=jnp.int32)[None, None, :]
    onehot = jnp.sum(matches.astype(jnp.int32), axis=1)
    weight = jnp.sum(
        jnp.where(matches, route_prob[:, :, None].astype(jnp.float32), jnp.float32(0.0)), axis=1
    )
    before = jnp.cumsum(onehot, axis=0) - onehot
    placing = (onehot.T[:, None, :] == 1) & (
        before.T[:, None, :] == jnp.arange(capacity, dtype=jnp.int32)[None, :, None]
    )
    return (onehot, weight, placing)


def on_device(attn_partial, hidden_in, norm_gain, expert_ids, route_prob, w_gate, w_up, w_down):
    experts = lax.axis_size("dp")
    dp_index = lax.axis_index("dp")
    tp_index = lax.axis_index("tp")
    partial_value = attn_partial[0].astype(jnp.float32)
    token_count = partial_value.shape[0]
    columns = hidden_in.shape[1]
    start_col = tp_index * columns
    own_cols = lax.dynamic_slice_in_dim(partial_value, start_col, columns, 1) + hidden_in.astype(
        jnp.float32
    )
    summand = lax.dynamic_update_slice_in_dim(partial_value, own_cols, start_col, 1)
    residual = lax.psum(summand, "tp")
    mean_sq = jnp.mean(residual * residual, axis=1, keepdims=True)
    normed = (residual * lax.rsqrt(mean_sq + eps) * norm_gain).astype(jnp.bfloat16)
    residual_cols = lax.dynamic_slice_in_dim(residual, start_col, columns, 1)
    onehot, weight, placing = route_tables(expert_ids, route_prob, experts, EXPERT_SLOTS)
    selection_mask = placing.reshape(experts * EXPERT_SLOTS, token_count).astype(jnp.bfloat16)
    outgoing = jnp.dot(selection_mask, normed, preferred_element_type=jnp.float32).astype(
        jnp.bfloat16
    )
    piece_width = outgoing.shape[1]
    incoming = lax.all_to_all(
        outgoing.reshape(experts, EXPERT_SLOTS, piece_width),
        "dp",
        split_axis=0,
        concat_axis=0,
        tiled=True,
    )
    expert_slot_rows = incoming.reshape(experts * EXPERT_SLOTS, piece_width)
    gate_val = jnp.dot(expert_slot_rows, w_gate[0], preferred_element_type=jnp.float32)
    up_val = jnp.dot(expert_slot_rows, w_up[0], preferred_element_type=jnp.float32)
    hidden_act = (jax.nn.silu(gate_val) * up_val).astype(jnp.bfloat16)
    partial_out = jnp.dot(hidden_act, w_down[0], preferred_element_type=jnp.float32)
    combine_matrix = (placing.astype(jnp.float32) * weight.T[:, None, :]).reshape(
        experts * EXPERT_SLOTS, token_count
    )
    expert_cols = lax.psum_scatter(
        partial_out.astype(jnp.bfloat16), "tp", scatter_dimension=1, tiled=True
    ).astype(jnp.float32)
    returned = lax.all_to_all(
        expert_cols.reshape(experts, EXPERT_SLOTS, columns).astype(jnp.bfloat16),
        "dp",
        split_axis=0,
        concat_axis=0,
        tiled=True,
    ).astype(jnp.float32)
    moe_out = jnp.dot(
        combine_matrix.T,
        returned.reshape(experts * EXPERT_SLOTS, columns),
        precision=lax.Precision.HIGHEST,
        preferred_element_type=jnp.float32,
    )
    layer_out = (residual_cols + moe_out).astype(jnp.bfloat16)
    hidden_peak = jnp.max(jnp.abs(hidden_act.astype(jnp.float32)))
    row_peak = jnp.max(jnp.abs(normed.astype(jnp.float32)), axis=1)
    local_entry = jnp.max(onehot.astype(jnp.float32) * row_peak[:, None], axis=0)
    own_slot = jnp.arange(experts, dtype=jnp.int32) == dp_index
    hidden_local = jnp.where(own_slot, hidden_peak, jnp.float32(0.0))
    every_entry, every_hidden = lax.pmax((local_entry, hidden_local), ("dp", "tp"))
    amax_input = lax.dynamic_slice_in_dim(every_entry, dp_index, 1, 0)
    amax_hidden = lax.dynamic_slice_in_dim(every_hidden, dp_index, 1, 0)
    return (layer_out, amax_input, amax_hidden)


def solution(mesh):
    placed = (
        P("tp", "dp", None),
        P("dp", "tp"),
        P(),
        P("dp", None),
        P("dp", None),
        P("dp", None, "tp"),
        P("dp", None, "tp"),
        P("dp", "tp", None),
    )
    return jax.shard_map(
        on_device,
        mesh=mesh,
        in_specs=placed,
        out_specs=(P("dp", "tp"), P("dp"), P("dp")),
        check_vma=False,
    )
```

profile of v0, /device:TPU:1, one launch (start us, length us, event | category | flops | bytes accessed | tf_op | source)
XLA Modules:
  0.0 342.8 jit_solution(10754556767076830818)
XLA Ops:
  7.2 0.0 copy-start.4
  7.2 0.0 all-reduce.3.cloned.1.call-start
  7.2 0.0 copy-start.6
  7.2 2.8 fusion.21
  10.1 0.0 copy-start.5
  10.1 0.0 copy-done.4
  10.1 1.1 fusion.14
  11.2 0.0 copy-start.1
  11.2 1.2 copy-done.1
  12.4 0.0 all-reduce.3.cloned.1.call-update
  12.4 0.0 reduce-scatter.2.cloned.1.call-start
  12.5 0.0 copy-done.6
  12.5 0.1 copy.26
  12.6 0.2 convert_reduce_fusion
  12.7 0.1 reduce_window_sum.11
  12.8 0.1 copy.28
  12.9 0.1 copy.27
  13.1 0.1 eq.64
  13.2 62.8 %all-reduce.3.cloned.1.call-done = f32[64,7168]{1,0:T(8,128)} async-done(((f32[64,7168]{1,0:T(8,128)}), f32[64,7168]{1,0:T(8,128)}) %all-reduce.3.cloned.1.call-update) | async-done | bytes 1835024 | tf_op jit(solution)/shard_map/psum | solution.py:35
  75.9 1.7 multiply_reduce_fusion
  77.7 0.0 copy-done.5
  77.7 4.5 %convolution_convert_fusion.1 = bf16[256,7168]{1,0:T(8,128)(2,1)} fusion(pred[256,64]{1,0:T(8,128)(4,1)S(1)} %bitcast.38, s32[256,64]{1,0:T(8,128)S(1)} %bitcast.37, s32[256]{0:T(256)S(1)} %eq.64, f32[64,7168]{1,0:T(8,128)} %all-reduce.3.cloned.1.call-done, f32[7168]{0:T(1024)S(1)} %copy-done.5, f32[64]{0:T(128)S(1)} %add_rsqrt_fusion), kind=kOutput, calls=%fused_computation.1 | convolution fusion | flops 238125056 | bytes 5616896 | tf_op jit(solution)/shard_map/dot_general | solution.py:41
  82.3 7.0 %reshape.39 = bf16[64,4,7168]{2,1,0:T(4,128)(2,1)} reshape(bf16[256,7168]{1,0:T(8,128)(2,1)} %convolution_convert_fusion.1) | data formatting | bytes 7340032 | tf_op jit(solution)/shard_map/reshape | solution.py:46
  89.3 94.8 %all_to_all.10 = bf16[64,4,7168]{2,1,0:T(4,128)(2,1)} all-to-all(bf16[64,4,7168]{2,1,0:T(4,128)(2,1)} %reshape.39), channel_id=1, replica_groups=mesh['dp'=64,'tp'=4] {'dp'}, dimensions={0} | all-to-all | bytes 7340032 | tf_op jit(solution)/shard_map/all_to_all | solution.py:45
  184.1 6.7 %reshape.40 = bf16[256,7168]{1,0:T(8,128)(2,1)} reshape(bf16[64,4,7168]{2,1,0:T(4,128)(2,1)} %all_to_all.10) | data formatting | bytes 7340032 | tf_op jit(solution)/shard_map/reshape | solution.py:52
  190.8 0.0 copy-start.3
  190.8 0.0 copy-start.8
  190.8 4.4 %fusion.3 = f32[256,256]{1,0:T(8,128)S(1)} fusion(bf16[256,7168]{1,0:T(8,128)(2,1)} %reshape.40, bf16[1,7168,256]{2,1,0:T(8,128)(2,1)} %param.13), kind=kOutput, calls=%fused_computation.5 | convolution fusion | flops 939524096 | bytes 7602176 | tf_op jit(solution)/shard_map/dot_general | solution.py:53
  195.2 0.0 copy-done.3
  195.2 0.9 copy-done.8
  196.1 0.0 copy-start.2
  196.1 1.7 abs_reduce_fusion.1
  197.9 0.3 copy-done.2
  198.2 2.9 convolution_convert_fusion
  201.1 0.0 copy-start.7
  201.1 0.0 copy-start
  201.1 0.0 reduce-scatter.2.cloned.1.call-update
  201.1 40.8 %reduce-scatter.2.cloned.1.call-done = bf16[256,1792]{1,0:T(8,128)(2,1)} async-done(((bf16[256,7168]{1,0:T(8,128)(2,1)}), bf16[256,1792]{1,0:T(8,128)(2,1)}) %reduce-scatter.2.cloned.1.call-update) | async-done | bytes 917520 | tf_op jit(solution)/shard_map/reduce_scatter | solution.py:60
  241.9 2.5 convert_element_type.57
  244.4 10.6 %all-to-all-start.1 = ((bf16[64,4,1792]{2,1,0:T(4,128)(2,1)}), bf16[64,4,1792]{2,1,0:T(4,128)(2,1)S(1)}, u32[]{:S(2)}, u32[]{:S(2)}) async-start(bf16[64,4,1792]{2,1,0:T(4,128)(2,1)} %convert_element_type.57), calls=%async_computation.2 | async-start | bytes 1835008 | tf_op jit(solution)/shard_map/all_to_all | solution.py:63
  255.1 0.0 copy-done.7
  255.1 0.1 copy.29
  255.2 0.2 select_reduce_fusion
  255.4 0.1 copy.30
  255.5 0.1 fusion.17
  255.5 0.0 copy-done
  255.5 0.4 abs_reduce_fusion
  255.9 0.1 multiply_reduce_fusion.1
  256.0 0.7 compare_select_fusion
  256.7 76.8 %all-reduce = (f32[64]{0:T(128)S(1)}, f32[64]{0:T(128)S(1)}) all-reduce(f32[64]{0:T(128)S(1)} %multiply_reduce_fusion.1, f32[64]{0:T(128)S(1)} %compare_select_fusion), channel_id=1, replica_groups=mesh['dp'=64,'tp'=4] {'dp','tp'}, use_global_device_ids=true, to_apply=%region_8.9 | all-reduce | flops 128 | bytes 1024 | tf_op jit(solution)/shard_map/pmax | solution.py:82
  333.5 0.6 dynamic_slice.18
  334.1 0.6 dynamic_slice.17
  334.7 0.0 all-to-all-done.1
  334.7 1.3 fusion.6
  (6 shorter events, 0.1 us)
Async XLA Ops:
  7.2 2.9 copy-start.4
  7.2 68.7 %all-reduce.3.cloned.1.call-start = ((), (), s32[]{:S(2)}) async-start(), calls=%async_computation.3 | async-start | bytes 3670016 | tf_op jit(solution)/shard_map/psum | solution.py:35
  7.2 5.3 %copy-start.6 = (s32[64,8]{0,1:T(8,128)S(1)}, s32[64,8]{0,1:T(8,128)}, u32[]{:S(2)}) copy-start(s32[64,8]{0,1:T(8,128)} %param.11) | copy-start | bytes 6148
  10.1 67.7 %copy-start.5 = (f32[7168]{0:T(1024)S(1)}, f32[7168]{0:T(1024)}, u32[]{:S(2)}) copy-start(f32[7168]{0:T(1024)} %param.10) | copy-start | bytes 86020
  11.2 1.3 copy-start.1
  12.4 229.5 %reduce-scatter.2.cloned.1.call-start = ((), (), s32[]{:S(2)}) async-start(), calls=%async_computation.4 | async-start | bytes 4587520 | tf_op jit(solution)/shard_map/reduce_scatter | solution.py:60
  190.8 4.4 %copy-start.3 = (bf16[256,7168]{1,0:T(8,128)(2,1)S(1)}, bf16[256,7168]{1,0:T(8,128)(2,1)}, u32[]{:S(2)}) copy-start(bf16[256,7168]{1,0:T(8,128)(2,1)} %reshape.40) | copy-start | bytes 11010052
  190.8 5.3 %copy-start.8 = (bf16[1,7168,256]{2,1,0:T(8,128)(2,1)S(1)}, bf16[1,7168,256]{2,1,0:T(8,128)(2,1)}, u32[]{:S(2)}) copy-start(bf16[1,7168,256]{2,1,0:T(8,128)(2,1)} %param.14) | copy-start | bytes 11010052
  196.1 2.0 copy-start.2
  201.1 54.0 %copy-start.7 = (bf16[64,8]{0,1:T(8,128)(2,1)S(1)}, bf16[64,8]{0,1:T(8,128)(2,1)}, u32[]{:S(2)}) copy-start(bf16[64,8]{0,1:T(8,128)(2,1)} %param.12) | copy-start | bytes 3076
  201.1 54.4 %copy-start = (f32[64,7168]{1,0:T(8,128)S(1)}, f32[64,7168]{1,0:T(8,128)}, u32[]{:S(2)}) copy-start(f32[64,7168]{1,0:T(8,128)} %all-reduce.3.cloned.1.call-done) | copy-start | bytes 5505028
  244.4 90.2 %all-to-all-start.1 = ((bf16[64,4,1792]{2,1,0:T(4,128)(2,1)}), bf16[64,4,1792]{2,1,0:T(4,128)(2,1)S(1)}, u32[]{:S(2)}, u32[]{:S(2)}) async-start(bf16[64,4,1792]{2,1,0:T(4,128)(2,1)} %convert_element_type.57), calls=%async_computation.2 | async-start | bytes 1835008 | tf_op jit(solution)/shard_map/all_to_all | solution.py:63
Sparse Core Ops, SparseCore 0:
  12.6 63.3 all-reduce.2
  201.2 40.6 reduce-scatter.1
where the time goes:
time: 344 us; the launch traced here: 343 us
  blocking collectives  172 us (50%)
  waiting for transfers between devices  104 us (30%)
  local copies, waits for them, and re-layouts  20.5 us (6%)
  matrix products  14.9 us (4%)
  between operations  14.2 us (4%)
  starting transfers between devices  10.7 us (3%)
  other arithmetic  7.3 us (2%)
    all_to_all x1, blocking collectives, on_device(): lax.all_to_all(outgoing.reshape(experts, EXPERT_SLOTS, piece_width), 'dp'...  94.8 us
    pmax x1, blocking collectives, on_device(): lax.pmax((local_entry, hidden_local), ('dp', 'tp'))  76.8 us
    psum x1, waiting for transfers between devices, on_device(): residual = lax.psum(summand, 'tp')  62.8 us
    reduce_scatter x1, waiting for transfers between devices, on_device(): lax.psum_scatter(partial_out.astype(jnp.bfloat16), 'tp', scatter_dimensio...  40.8 us
    all_to_all x1, starting transfers between devices, on_device(): lax.all_to_all(expert_cols.reshape(experts, EXPERT_SLOTS, columns).astype...  10.6 us
    reshape x1, local copies, waits for them, and re-layouts, on_device(): outgoing.reshape(experts, EXPERT_SLOTS, piece_width)  7 us
  transfers between devices with their start and end apart: 3, of which 2 were waited for; matrix products, arithmetic and copies ran while one was open for 1% of the time, Pallas kernels for 0%

commit v1 on v0

--- a/solution.py
+++ b/solution.py
@@ -32,7 +32,7 @@
         jnp.float32
     )
     summand = lax.dynamic_update_slice_in_dim(partial_value, own_cols, start_col, 1)
-    residual = lax.psum(summand, "tp")
+    residual = jnp.sum(lax.all_gather(summand, "tp"), axis=0)
     mean_sq = jnp.mean(residual * residual, axis=1, keepdims=True)
     normed = (residual * lax.rsqrt(mean_sq + eps) * norm_gain).astype(jnp.bfloat16)
     residual_cols = lax.dynamic_slice_in_dim(residual, start_col, columns, 1)

time: 344 us -> 360 us (1.047)
  waiting for transfers between devices: 104 us -> 122 us
    all_gather x0 -> x1, waiting for transfers between devices: none -> 80.1 us  [on_device(): residual = jnp.sum(lax.all_gather(summand, 'tp'), axis=0)]
    psum x1 -> x0, waiting for transfers between devices: 62.8 us -> none  [on_device(): residual = lax.psum(summand, 'tp')]
    reduce_sum x0 -> x1, other arithmetic: none -> 3.7 us  [on_device(): residual = jnp.sum(lax.all_gather(summand, 'tp'), axis=0)]
where the time goes in v1:
time: 360 us
  blocking collectives  172 us (48%)
  waiting for transfers between devices  122 us (34%)
  local copies, waits for them, and re-layouts  20.6 us (6%)
  between operations  14.2 us (4%)
  matrix products  13.4 us (4%)
  starting transfers between devices  10.7 us (3%)
  other arithmetic  7.02 us (2%)
    all_to_all x1, blocking collectives, on_device(): lax.all_to_all(outgoing.reshape(experts, EXPERT_SLOTS, piece_width), 'dp'...  94.9 us
    all_gather x1, waiting for transfers between devices, on_device(): residual = jnp.sum(lax.all_gather(summand, 'tp'), axis=0)  80.1 us
    pmax x1, blocking collectives, on_device(): lax.pmax((local_entry, hidden_local), ('dp', 'tp'))  76.8 us
    reduce_scatter x1, waiting for transfers between devices, on_device(): lax.psum_scatter(partial_out.astype(jnp.bfloat16), 'tp', scatter_dimensio...  41.8 us
    all_to_all x1, starting transfers between devices, on_device(): lax.all_to_all(expert_cols.reshape(experts, EXPERT_SLOTS, columns).astype...  10.7 us
  transfers between devices with their start and end apart: 3, of which 2 were waited for; matrix products, arithmetic and copies ran while one was open for 1% of the time, Pallas kernels for 0%

profile of v1, /device:TPU:1, one launch (start us, length us, event | category | flops | bytes accessed | tf_op | source)
XLA Modules:
  0.0 359.6 jit_solution(13948237876427220122)
XLA Ops:
  7.2 0.0 copy-start.3
  7.2 0.0 copy-start.5
  7.2 0.0 all-gather.2.cloned.1.call-start
  7.2 1.4 convert_element_type.47
  8.6 0.0 copy-done.3
  8.6 0.1 bitcast_dynamic-update-slice_fusion
  8.7 0.0 copy-start
  8.7 1.3 copy-done
  10.0 0.0 all-gather.2.cloned.1.call-update
  10.1 0.0 reduce-scatter.2.cloned.1.call-start
  10.1 0.0 copy-done.5
  10.1 0.1 copy.26
  10.2 0.2 convert_reduce_fusion
  10.4 0.1 reduce_window_sum.11
  10.5 0.1 copy.28
  10.6 0.1 copy.27
  10.7 0.1 eq.64
  10.8 0.0 copy-start.4
  10.8 80.1 %all-gather.2.cloned.1.call-done = f32[4,64,7168]{2,1,0:T(8,128)} async-done(((f32[1,64,7168]{2,1,0:T(8,128)}), f32[4,64,7168]{2,1,0:T(8,128)}) %all-gather.2.cloned.1.call-update) | async-done | bytes 7340048 | tf_op jit(solution)/shard_map/all_gather | solution.py:35
  90.9 3.7 %reduce_sum.36 = f32[64,7168]{1,0:T(8,128)S(1)} reduce(f32[4,64,7168]{2,1,0:T(8,128)} %all-gather.2.cloned.1.call-done, f32[]{:T(128)} %constant.28.clone.1), dimensions={0}, to_apply=%region_0.0 | reduce | flops 1376256 | bytes 9175044 | tf_op jit(solution)/shard_map/reduce_sum | solution.py:35
  94.6 0.2 multiply_reduce_fusion
  94.9 0.0 copy-done.4
  95.0 3.0 convolution_convert_fusion.1
  98.0 7.0 %reshape.41 = bf16[64,4,7168]{2,1,0:T(4,128)(2,1)} reshape(bf16[256,7168]{1,0:T(8,128)(2,1)} %convolution_convert_fusion.1) | data formatting | bytes 7340032 | tf_op jit(solution)/shard_map/reshape | solution.py:46
  105.0 94.9 %all_to_all.10 = bf16[64,4,7168]{2,1,0:T(4,128)(2,1)} all-to-all(bf16[64,4,7168]{2,1,0:T(4,128)(2,1)} %reshape.41), channel_id=1, replica_groups=mesh['dp'=64,'tp'=4] {'dp'}, dimensions={0} | all-to-all | bytes 7340032 | tf_op jit(solution)/shard_map/all_to_all | solution.py:45
  199.8 6.7 %reshape.42 = bf16[256,7168]{1,0:T(8,128)(2,1)} reshape(bf16[64,4,7168]{2,1,0:T(4,128)(2,1)} %all_to_all.10) | data formatting | bytes 7340032 | tf_op jit(solution)/shard_map/reshape | solution.py:52
  206.6 0.0 copy-start.2
  206.6 0.0 copy-start.7
  206.6 4.4 %fusion.3 = f32[256,256]{1,0:T(8,128)S(1)} fusion(bf16[256,7168]{1,0:T(8,128)(2,1)} %reshape.42, bf16[1,7168,256]{2,1,0:T(8,128)(2,1)} %param.13), kind=kOutput, calls=%fused_computation.5 | convolution fusion | flops 939524096 | bytes 7602176 | tf_op jit(solution)/shard_map/dot_general | solution.py:53
  211.0 0.0 copy-done.2
  211.0 0.9 copy-done.7
  211.9 0.0 copy-start.1
  211.9 1.7 abs_reduce_fusion.1
  213.6 0.3 copy-done.1
  213.9 2.9 convolution_convert_fusion
  216.8 0.0 copy-start.6
  216.8 0.0 reduce-scatter.2.cloned.1.call-update
  216.9 41.8 %reduce-scatter.2.cloned.1.call-done = bf16[256,1792]{1,0:T(8,128)(2,1)} async-done(((bf16[256,7168]{1,0:T(8,128)(2,1)}), bf16[256,1792]{1,0:T(8,128)(2,1)}) %reduce-scatter.2.cloned.1.call-update) | async-done | bytes 917520 | tf_op jit(solution)/shard_map/reduce_scatter | solution.py:60
  258.7 2.5 convert_element_type.55
  261.2 10.7 %all-to-all-start.1 = ((bf16[64,4,1792]{2,1,0:T(4,128)(2,1)}), bf16[64,4,1792]{2,1,0:T(4,128)(2,1)S(1)}, u32[]{:S(2)}, u32[]{:S(2)}) async-start(bf16[64,4,1792]{2,1,0:T(4,128)(2,1)} %convert_element_type.55), calls=%async_computation.2 | async-start | bytes 1835008 | tf_op jit(solution)/shard_map/all_to_all | solution.py:63
  271.8 0.0 copy-done.6
  271.9 0.1 copy.29
  271.9 0.2 select_reduce_fusion
  272.2 0.1 copy.30
  272.2 0.1 fusion.16
  272.3 0.4 abs_reduce_fusion
  272.7 0.1 multiply_reduce_fusion.1
  272.8 0.7 compare_select_fusion
  273.4 76.8 %all-reduce = (f32[64]{0:T(128)S(1)}, f32[64]{0:T(128)S(1)}) all-reduce(f32[64]{0:T(128)S(1)} %multiply_reduce_fusion.1, f32[64]{0:T(128)S(1)} %compare_select_fusion), channel_id=1, replica_groups=mesh['dp'=64,'tp'=4] {'dp','tp'}, use_global_device_ids=true, to_apply=%region_8.9 | all-reduce | flops 128 | bytes 1024 | tf_op jit(solution)/shard_map/pmax | solution.py:82
  350.3 0.6 dynamic_slice.18
  350.9 0.6 dynamic_slice.17
  351.4 0.0 all-to-all-done.1
  351.4 1.3 fusion.6
  (7 shorter events, 0.1 us)
Async XLA Ops:
  7.2 1.5 copy-start.3
  7.2 2.9 copy-start.5
  7.2 83.7 %all-gather.2.cloned.1.call-start = ((), (), s32[]{:S(2)}) async-start(), calls=%async_computation.3 | async-start | bytes 9175040 | tf_op jit(solution)/shard_map/all_gather | solution.py:35
  8.7 1.3 copy-start
  10.1 248.6 %reduce-scatter.2.cloned.1.call-start = ((), (), s32[]{:S(2)}) async-start(), calls=%async_computation.4 | async-start | bytes 4587520 | tf_op jit(solution)/shard_map/reduce_scatter | solution.py:60
  10.8 84.2 %copy-start.4 = (f32[7168]{0:T(1024)S(1)}, f32[7168]{0:T(1024)}, u32[]{:S(2)}) copy-start(f32[7168]{0:T(1024)} %param.10) | copy-start | bytes 86020
  206.6 4.4 %copy-start.2 = (bf16[256,7168]{1,0:T(8,128)(2,1)S(1)}, bf16[256,7168]{1,0:T(8,128)(2,1)}, u32[]{:S(2)}) copy-start(bf16[256,7168]{1,0:T(8,128)(2,1)} %reshape.42) | copy-start | bytes 11010052
  206.6 5.3 %copy-start.7 = (bf16[1,7168,256]{2,1,0:T(8,128)(2,1)S(1)}, bf16[1,7168,256]{2,1,0:T(8,128)(2,1)}, u32[]{:S(2)}) copy-start(bf16[1,7168,256]{2,1,0:T(8,128)(2,1)} %param.14) | copy-start | bytes 11010052
  211.9 2.0 copy-start.1
  216.8 55.0 %copy-start.6 = (bf16[64,8]{0,1:T(8,128)(2,1)S(1)}, bf16[64,8]{0,1:T(8,128)(2,1)}, u32[]{:S(2)}) copy-start(bf16[64,8]{0,1:T(8,128)(2,1)} %param.12) | copy-start | bytes 3076
  261.2 90.3 %all-to-all-start.1 = ((bf16[64,4,1792]{2,1,0:T(4,128)(2,1)}), bf16[64,4,1792]{2,1,0:T(4,128)(2,1)S(1)}, u32[]{:S(2)}, u32[]{:S(2)}) async-start(bf16[64,4,1792]{2,1,0:T(4,128)(2,1)} %convert_element_type.55), calls=%async_computation.2 | async-start | bytes 1835008 | tf_op jit(solution)/shard_map/all_to_all | solution.py:63
Sparse Core Ops, SparseCore 0:
  10.2 80.6 all-gather.1
  217.0 41.6 reduce-scatter.1
